TPU v7x, 128 devices: a whole 4x4x4 slice. The times are simulated.
128 devices in a mesh: ep: 4 (over x), tm: 32 (over y, z, core).
Axes of the slice: x: 4, y: 4, z: 4, core: 2. Of those that a mesh axis runs over, the one named last changes fastest.
Arguments:
- predictions: float32 [128, 1048576], P('ep', 'tm'), may hold values from -6 to 6
- leaf_index: int32 [128, 1048576], P('ep', 'tm'), may hold values from 0 to 63
- events: int32 [128, 1048576], P('ep', 'tm'), may hold values 0 or 1
- tie_start: int32 [1048576], P('tm'), may hold values from 0 to 1, as said below
Outputs:
- new_pred: float32 [128, 1048576], P('ep', 'tm')
- leaf_weights: float32 [128, 64], P('ep')
- grad_hess: bfloat16 [2, 128, 32, 32768], P(None, None, 'tm', 'ep')
Inputs may be any that keep to these rules, and one draw needn't show every extreme that they name: `tie_start`: every row whose index is a multiple of 128 begins a tie group.
All inputs are finite; a program needn't handle non-finite values. No bound on the sum of `events` on one device may be relied on, other than what follows from the above.
Results may differ from a plain program's by a relative error of at most 0.0023.
Values may be sent and summed in bfloat16 or wider, within the bound.
A program may use at most 128 MiB of HBM per device.

v0:
```python
import math
import jax
import jax.numpy as jnp
from jax import lax
from jax.sharding import PartitionSpec as P

LEAVES = 64


def prefix(part, axis, combine, identity, reverse):
    count = lax.axis_size(axis)
    place = lax.axis_index(axis)
    ahead = count - 1 - place if reverse else place
    gathered = jax.tree.map(lambda a: lax.all_gather(a, axis), part)
    state = jax.tree.map(lambda a, e: jnp.zeros_like(a) + jnp.asarray(e, a.dtype), part, identity)

    def one(turn, state):
        source = count - 1 - turn if reverse else turn
        return combine(
            state, jax.tree.map(lambda a: lax.dynamic_index_in_dim(a, source, 0, False), gathered)
        )

    return lax.fori_loop(0, ahead, one, state)


def tile_matrices(tie_start):
    length = tie_start.shape[0]
    blocks = length // 128
    starts = tie_start.reshape(blocks, 128)
    labels = jnp.arange(128, dtype=jnp.int32)
    first_local = lax.cummax(jnp.where(starts == 1, labels[None, :], 0), axis=1)
    next_start = jnp.concatenate([starts[:, 1:], jnp.ones((blocks, 1), jnp.int32)], axis=1)
    last_local = lax.cummin(jnp.where(next_start == 1, labels[None, :], 127), axis=1, reverse=True)
    backward = (labels[None, :, None] >= first_local[:, None, :]).astype(jnp.float32)
    forward = (labels[None, :, None] <= last_local[:, None, :]).astype(jnp.float32)
    return (backward, forward)


def block_cumsum(values, matrices, from_end):
    groups = values.shape[0]
    length = values.shape[1]
    blocks = length // 128
    shaped = values.reshape(groups, blocks, 128)
    within = jnp.einsum("ebj,bji->ebi", shaped, matrices, precision=lax.Precision.HIGHEST)
    totals = jnp.sum(shaped, axis=2)
    if from_end:
        offsets = jnp.cumsum(totals[:, ::-1], axis=1)[:, ::-1] - totals
    else:
        offsets = jnp.cumsum(totals, axis=1) - totals
    return (within + offsets[:, :, None]).reshape(groups, length)


def add_values(earlier, later):
    return jax.tree.map(lambda left, right: left + right, earlier, later)


def leaf_partials(leaf_index, gradient, hessian, leaves):
    length = leaf_index.shape[1]
    width = math.gcd(length, 2048)
    labels = jnp.arange(leaves, dtype=jnp.int32)

    def one_block(step, totals):
        start = step * width
        part_leaf = lax.dynamic_slice_in_dim(leaf_index, start, width, 1)
        part_grad = lax.dynamic_slice_in_dim(gradient, start, width, 1)
        part_hess = lax.dynamic_slice_in_dim(hessian, start, width, 1)
        hits = part_leaf[:, None, :] == labels[None, :, None]
        gsum = jnp.sum(jnp.where(hits, part_grad[:, None, :], 0.0), axis=2)
        hsum = jnp.sum(jnp.where(hits, part_hess[:, None, :], 0.0), axis=2)
        return totals + jnp.stack([gsum, hsum], axis=1)

    empty = jnp.zeros((leaf_index.shape[0], 2, leaves), jnp.float32)
    return lax.fori_loop(0, length // width, one_block, empty)


def leaf_lookup(leaf_index, table):
    length = leaf_index.shape[1]
    width = math.gcd(length, 2048)
    labels = jnp.arange(table.shape[1], dtype=jnp.int32)

    def one_block(step, result):
        start = step * width
        part_leaf = lax.dynamic_slice_in_dim(leaf_index, start, width, 1)
        hits = part_leaf[:, None, :] == labels[None, :, None]
        picked = jnp.sum(jnp.where(hits, table[:, :, None], 0.0), axis=1)
        return lax.dynamic_update_slice_in_dim(result, picked, start, 1)

    empty = jnp.zeros(leaf_index.shape, jnp.float32)
    return lax.fori_loop(0, length // width, one_block, empty)


def on_device(predictions, leaf_index, events, tie_start):
    groups = predictions.shape[0]
    length = predictions.shape[1]
    backward, forward = tile_matrices(tie_start)
    weight = jnp.exp(predictions)
    local_risk = block_cumsum(weight, backward, True)
    block_total = local_risk[:, 0]
    zero_column = jnp.zeros((groups,), jnp.float32)
    later_total = prefix(block_total, "tm", add_values, zero_column, True)
    risk = local_risk + later_total[:, None]
    observed = events.astype(jnp.float32)
    inv_one = observed / risk
    inv_two = inv_one / risk
    local_one = block_cumsum(inv_one, forward, False)
    local_two = block_cumsum(inv_two, forward, False)
    totals_pair = (local_one[:, -1], local_two[:, -1])
    earlier_one, earlier_two = prefix(
        totals_pair, "tm", add_values, (zero_column, zero_column), False
    )
    accum_one = local_one + earlier_one[:, None]
    accum_two = local_two + earlier_two[:, None]
    gradient = weight * accum_one - observed
    hessian = weight * accum_one - weight * weight * accum_two
    stacked = jnp.stack([gradient, hessian]).astype(jnp.bfloat16).reshape(2, groups, 1, length)
    grad_hess = lax.all_to_all(stacked, "ep", split_axis=3, concat_axis=1, tiled=True)
    partial_value = leaf_partials(leaf_index, gradient, hessian, LEAVES)
    totals = lax.psum(partial_value, "tm")
    leaf_weights = -totals[:, 0] / (totals[:, 1] + 1.0)
    new_pred = predictions + leaf_lookup(leaf_index, leaf_weights)
    return (new_pred, leaf_weights, grad_hess)


def solution(mesh):
    placed = (P("ep", "tm"), P("ep", "tm"), P("ep", "tm"), P("tm"))
    return jax.shard_map(
        on_device,
        mesh=mesh,
        in_specs=placed,
        out_specs=(P("ep", "tm"), P("ep", None), P(None, None, "tm", "ep")),
        check_vma=False,
    )
```

profile of v0, /device:TPU:2, one launch (start us, length us, event | category | flops | bytes accessed | tf_op | source)
XLA Modules:
  0.0 666.5 jit_solution(1025747727024494581)
XLA Ops:
  0.6 6.2 exponential_bitcast_fusion.1
  7.2 2.9 copy.163
  10.1 1.1 bitcast_reduce_fusion.2
  12.6 10.0 %fusion.22 = f32[256,4,8,128]{3,2,1,0:T(8,128)S(1)} fusion(f32[4,256,8,128]{3,2,1,0:T(8,128)} %get-tuple-element.397, s32[256,128]{1,0:T(8,128)S(1)} %copy.130, f32[32,256]{0,1:T(8,128)S(1)} %copy.134), kind=kOutput, calls=%fused_computation.44 | convolution fusion | flops 1615855616 | bytes 8552448 | tf_op jit(solution)/shard_map/ebj,bji->ebi/dot_general | solution.py:44
  22.9 1.7 copy-done.1
  26.2 68.6 %all-reduce.1 = f32[1024]{0:T(1024)S(1)} all-reduce(f32[1024]{0:T(1024)S(1)} %dynamic-update-slice), channel_id=2, replica_groups=mesh['ep'=4,'tm'=32] {'tm'}, use_global_device_ids=true, to_apply=%add.1 | all-reduce | flops 1024 | bytes 8192
  94.9 1.3 while.52
  96.5 4.4 reduce_window_min.10
  101.0 9.3 %fusion.34 = (f32[4,8,256,128]{3,1,2,0:T(8,128)}, f32[4,256,8,128]{3,2,1,0:T(8,128)}, f32[4,256,8,128]{3,2,1,0:T(8,128)}, f32[4,8,256,128]{3,1,2,0:T(8,128)S(1)}) fusion(f32[32]{0:T(128)S(1)} %get-tuple-element.296, f32[256,4,8,128]{3,2,1,0:T(8,128)} %copy-done.1, s32[32,32768]{1,0:T(8,128)} %param.14), kind=kLoop, calls=%fused_computation.79 | loop fusion | flops 5242880 | bytes 25165952
  111.0 1.1 bitcast_reduce_fusion.1
  113.4 10.0 %fusion.21 = f32[256,4,8,128]{3,2,1,0:T(8,128)S(1)} fusion(f32[4,256,8,128]{3,2,1,0:T(8,128)} %get-tuple-element.394, s32[256,128]{1,0:T(8,128)S(1)} %copy.128, f32[32,256]{0,1:T(8,128)S(1)} %copy.139), kind=kOutput, calls=%fused_computation.42 | convolution fusion | flops 1615855616 | bytes 8552448 | tf_op jit(solution)/shard_map/ebj,bji->ebi/dot_general | solution.py:44
  123.7 1.8 copy-done
  125.7 1.4 copy-done.3
  127.8 1.1 bitcast_reduce_fusion
  130.0 10.0 %fusion.20 = f32[256,4,8,128]{3,2,1,0:T(8,128)S(1)} fusion(f32[4,256,8,128]{3,2,1,0:T(8,128)} %get-tuple-element.393, s32[256,128]{1,0:T(8,128)S(1)} %copy.128, f32[32,256]{0,1:T(8,128)S(1)} %copy.144), kind=kOutput, calls=%fused_computation.40 | convolution fusion | flops 1615855616 | bytes 8552448 | tf_op jit(solution)/shard_map/ebj,bji->ebi/dot_general | solution.py:44
  140.3 1.7 copy-done.2
  142.7 64.1 %all-reduce.4 = (f32[1024]{0:T(1024)S(1)}, f32[1024]{0:T(1024)S(1)}) all-reduce(f32[1024]{0:T(1024)S(1)} %dynamic-update-slice.1, f32[1024]{0:T(1024)S(1)} %dynamic-update-slice.2), channel_id=3, replica_groups=mesh['ep'=4,'tm'=32] {'tm'}, use_global_device_ids=true, to_apply=%add.2 | all-reduce | flops 2048 | bytes 16384
  206.9 10.2 %convert_bitcast_fusion = (bf16[1,32,1,32768]{3,1,2,0:T(8,128)(2,1)S(1)}, f32[32,32768]{1,0:T(8,128)}, bf16[1,32,1,32768]{3,1,2,0:T(8,128)(2,1)S(1)}, f32[32,32768]{1,0:T(8,128)}) fusion(f32[32]{0:T(128)S(1)} %get-tuple-element.298, f32[256,4,8,128]{3,2,1,0:T(8,128)} %copy-done.2, f32[32]{0:T(128)S(1)} %get-tuple-element.297, f32[256,4,8,128]{3,2,1,0:T(8,128)} %copy-done, ...), kind=kLoop, calls=%fused_computation.52 | loop fusion | flops 10485760 | bytes 29360384 | tf_op jit(solution)/shard_map/stack | solution.py:115
  217.1 2.4 pad_maximum_fusion
  219.5 33.0 %copy.146 = bf16[2,32,1,32768]{1,0,2,3:T(2,128)(2,1)} copy(bf16[2,32,1,32768]{3,1,2,0:T(8,128)(2,1)} %pad_maximum_fusion) | data formatting | bytes 8388608 | tf_op jit(solution)/shard_map/stack | solution.py:115
  252.5 19.2 %reshape.184 = bf16[4,2,262144]{2,1,0:T(2,128)(2,1)} reshape(bf16[32768,1,2,32]{3,2,1,0:T(2,128)(2,1)} %bitcast.143) | data formatting | bytes 8388608
  271.7 5.3 all-to-all-start
  277.1 117.7 %while.55 = (s32[]{:T(128)}, f32[32,2,64]{2,0,1:T(8,128)S(1)}, s32[32,32768]{1,0:T(8,128)}, f32[32,32768]{1,0:T(8,128)}, f32[32,32768]{1,0:T(8,128)}, /*index=5*/s32[]{:T(128)}, s32[]{:T(128)}, s32[]{:T(128)}, s32[]{:T(128)}) while((s32[]{:T(128)}, f32[32,2,64]{2,0,1:T(8,128)S(1)}, s32[32,32768]{1,0:T(8,128)}, ...), condition=%wide.region_18.19_spmd.clone, body=%wide.region_15.18_spmd.clone.sunk | while | flops 20979716 | bytes 2424997 | solution.py:73
  279.1 5.3 fusion.39
  284.4 1.1 constant_dynamic-slice_fusion.8
  286.5 5.3 fusion.39
  291.8 1.1 constant_dynamic-slice_fusion.8
  293.8 5.3 fusion.39
  301.2 5.3 fusion.39
  308.5 5.3 fusion.39
  315.9 5.3 fusion.39
  323.2 5.3 fusion.39
  330.6 5.3 fusion.39
  337.9 5.3 fusion.39
  345.3 5.3 fusion.39
  352.7 5.3 fusion.39
  360.0 5.3 fusion.39
  367.4 5.3 fusion.39
  374.7 5.3 fusion.39
  382.1 5.3 fusion.39
  389.4 5.3 fusion.39
  394.7 124.3 %psum.7 = f32[32,2,64]{2,0,1:T(8,128)S(1)} all-reduce(f32[32,2,64]{2,0,1:T(8,128)S(1)} %get-tuple-element.299), channel_id=1, replica_groups=mesh['ep'=4,'tm'=32] {'tm'}, use_global_device_ids=true, to_apply=%region_19.20 | all-reduce | flops 4096 | bytes 32768 | tf_op jit(solution)/shard_map/psum | solution.py:118
  519.1 2.3 broadcast_in_dim.125
  521.3 80.5 %while.54 = (s32[]{:T(128)}, f32[32,32768]{1,0:T(8,128)}, s32[32,32768]{1,0:T(8,128)}, f32[32,64]{1,0:T(8,128)S(1)}, s32[]{:T(128)}, /*index=5*/s32[]{:T(128)}, s32[]{:T(128)}, s32[]{:T(128)}) while((s32[]{:T(128)}, f32[32,32768]{1,0:T(8,128)}, s32[32,32768]{1,0:T(8,128)}, f32[32,64]{1,0:T(8,128)S(1)}, s32[]{:T(128)}, ...), condition=%wide.region_22.23_spmd.clone, body=%wide.region_20.22_spmd.clone.sunk | while | flops 12517382 | bytes 1581203 | solution.py:89
  522.3 3.3 select_reduce_fusion.2
  527.3 3.3 select_reduce_fusion.2
  532.4 3.3 select_reduce_fusion.2
  537.4 3.3 select_reduce_fusion.2
  542.4 3.3 select_reduce_fusion.2
  547.5 3.3 select_reduce_fusion.2
  552.5 3.3 select_reduce_fusion.2
  557.5 3.3 select_reduce_fusion.2
  562.6 3.3 select_reduce_fusion.2
  567.6 3.3 select_reduce_fusion.2
  572.6 3.3 select_reduce_fusion.2
  577.6 3.3 select_reduce_fusion.2
  582.7 3.3 select_reduce_fusion.2
  587.7 3.3 select_reduce_fusion.2
  592.7 3.3 select_reduce_fusion.2
  597.8 3.3 select_reduce_fusion.2
  601.8 5.9 add.165
  607.7 12.0 %reshape.185 = bf16[32768,1,2,32]{3,2,1,0:T(2,128)(2,1)} reshape(bf16[4,2,262144]{2,1,0:T(2,128)(2,1)} %all-to-all-done) | data formatting | bytes 8388608
  619.7 40.0 %copy.150 = bf16[2,32,1,4,8192]{4,3,1,0,2:T(4,128)(2,1)} copy(bf16[2,32,1,4,8192]{1,0,4,3,2:T(2,128)(2,1)} %bitcast.144) | data formatting | bytes 8388608 | tf_op jit(solution)/shard_map/all_to_all | solution.py:116
  659.8 6.5 copy.148
  (176 shorter events, 66.8 us)
Async XLA Ops:
  0.6 6.2 copy-start.5
  22.6 2.0 copy-start.1
  22.6 2.1 copy-start.6
  123.4 2.1 copy-start
  123.4 3.7 copy-start.3
  140.0 2.0 copy-start.2
  271.7 336.0 %all-to-all-start = ((bf16[4,2,262144]{2,1,0:T(2,128)(2,1)}), bf16[4,2,262144]{2,1,0:T(2,128)(2,1)}, u32[]{:S(2)}, u32[]{:S(2)}) async-start(bf16[4,2,262144]{2,1,0:T(2,128)(2,1)} %reshape.184), calls=%async_computation | async-start | bytes 8388608 | tf_op jit(solution)/shard_map/all_to_all | solution.py:116
  601.8 5.9 copy-start.4
where the time goes:
time: 677 us; the launch traced here: 666 us
  blocking collectives  257 us (38%)
  local copies, waits for them, and re-layouts  195 us (29%)
  other arithmetic  176 us (26%)
  matrix products  30 us (4%)
    unnamed x2, blocking collectives  133 us
    psum x1, blocking collectives, on_device(): totals = lax.psum(partial_value, 'tm')  124 us
    reduce_sum x16, other arithmetic, one_block(): gsum = jnp.sum(jnp.where(hits, part_grad[:, None, :], 0.0), axis=2)  84.3 us
    reduce_sum x16, other arithmetic, one_block(): picked = jnp.sum(jnp.where(hits, table[:, :, None], 0.0), axis=1)  53.2 us
    unnamed x27, local copies, waits for them, and re-layouts  49.8 us
    all_to_all x2, local copies, waits for them, and re-layouts, on_device(): lax.all_to_all(stacked, 'ep', split_axis=3, concat_axis=1, tiled=True)  46.5 us
    another operation x1, local copies, waits for them, and re-layouts, on_device(): jnp.stack([gradient, hessian]).astype(jnp.bfloat16)  33 us
    dynamic_slice x32, local copies, waits for them, and re-layouts, one_block(): part_leaf = lax.dynamic_slice_in_dim(leaf_index, start, width, 1)  31.1 us
  transfers between devices with their start and end apart: 1, of which 0 were waited for; matrix products, arithmetic and copies ran while one was open for 31% of the time, Pallas kernels for 0%

commit v1 on v0

--- a/solution.py
+++ b/solution.py
@@ -5,6 +5,22 @@
 from jax.sharding import PartitionSpec as P
 
 LEAVES = 64
+
+
+def swapped_with_each(x, axis, split, join):
+    ways, here = (lax.axis_size(axis), lax.axis_index(axis))
+    width = x.shape[split] // ways
+    dims = list(x.shape)
+    dims[split] = width
+    height = dims[join]
+    dims[join] = height * ways
+    full = jnp.zeros(dims, x.dtype)
+    for mask in range(ways):
+        part = lax.dynamic_slice_in_dim(x, (here ^ mask) * width, width, axis=split)
+        if mask:
+            part = lax.ppermute(part, axis, [(d, d ^ mask) for d in range(ways)])
+        full = lax.dynamic_update_slice_in_dim(full, part, (here ^ mask) * height, axis=join)
+    return full
 
 
 def prefix(part, axis, combine, identity, reverse):
@@ -113,7 +129,7 @@
     gradient = weight * accum_one - observed
     hessian = weight * accum_one - weight * weight * accum_two
     stacked = jnp.stack([gradient, hessian]).astype(jnp.bfloat16).reshape(2, groups, 1, length)
-    grad_hess = lax.all_to_all(stacked, "ep", split_axis=3, concat_axis=1, tiled=True)
+    grad_hess = swapped_with_each(stacked, "ep", 3, 1)
     partial_value = leaf_partials(leaf_index, gradient, hessian, LEAVES)
     totals = lax.psum(partial_value, "tm")
     leaf_weights = -totals[:, 0] / (totals[:, 1] + 1.0)

time: 677 us -> 571 us (0.84)
  local copies, waits for them, and re-layouts: 195 us -> 88.3 us
    all_to_all x2 -> x0, local copies, waits for them, and re-layouts: 46.5 us -> none  [on_device(): lax.all_to_all(stacked, 'ep', split_axis=3, concat_axis=1, tiled=True)]
    unnamed x27, local copies, waits for them, and re-layouts: 49.8 us -> 15 us
    another operation x8 -> x7, local copies, waits for them, and re-layouts: 33.4 us -> 0.34 us  [the longest x1 33 us: on_device(): jnp.stack([gradient, hessian]).astype(jnp.bfloat16)]
  transfers between devices with their start and end apart: 1 -> 3, of which waited for: 0 -> 0; matrix products, arithmetic and copies ran while one was open for 31% -> 38% of each run, Pallas kernels for 0% -> 0%
where the time goes in v1:
time: 571 us; the launch traced here: 560 us
  blocking collectives  256 us (45%)
  other arithmetic  179 us (31%)
  local copies, waits for them, and re-layouts  88.3 us (15%)
  matrix products  30.1 us (5%)
    unnamed x2, blocking collectives  132 us
    psum x1, blocking collectives, on_device(): totals = lax.psum(partial_value, 'tm')  124 us
    reduce_sum x16, other arithmetic, one_block(): gsum = jnp.sum(jnp.where(hits, part_grad[:, None, :], 0.0), axis=2)  84.3 us
    reduce_sum x16, other arithmetic, one_block(): picked = jnp.sum(jnp.where(hits, table[:, :, None], 0.0), axis=1)  53.2 us
    dynamic_slice x32, local copies, waits for them, and re-layouts, one_block(): part_leaf = lax.dynamic_slice_in_dim(leaf_index, start, width, 1)  31.1 us
    dot_general x3, matrix products, block_cumsum(): jnp.einsum('ebj,bji->ebi', shaped, matrices, precision=lax.Precision.HIGH...  30.1 us
    dynamic_slice x16, local copies, waits for them, and re-layouts, one_block(): part_hess = lax.dynamic_slice_in_dim(hessian, start, width, 1)  17.1 us
    unnamed x27, local copies, waits for them, and re-layouts  15 us
  transfers between devices with their start and end apart: 3, of which 0 were waited for; matrix products, arithmetic and copies ran while one was open for 38% of the time, Pallas kernels for 0%

profile of v1, /device:TPU:2, one launch (start us, length us, event | category | flops | bytes accessed | tf_op | source)
XLA Modules:
  0.0 560.4 jit_solution(15467167268529573484)
XLA Ops:
  0.7 4.7 exponential_bitcast_fusion.1
  6.2 1.1 bitcast_reduce_fusion.2
  9.0 10.0 %fusion.22 = f32[256,4,8,128]{3,2,1,0:T(8,128)S(1)} fusion(f32[4,256,8,128]{3,2,1,0:T(8,128)} %get-tuple-element.391, s32[256,128]{1,0:T(8,128)S(1)} %copy.36, f32[32,256]{0,1:T(8,128)S(1)} %copy.40), kind=kOutput, calls=%fused_computation.51 | convolution fusion | flops 1615855616 | bytes 8552448 | tf_op jit(solution)/shard_map/ebj,bji->ebi/dot_general | solution.py:60
  19.3 1.7 copy-done.3
  22.7 68.6 %all-reduce.1 = f32[1024]{0:T(1024)S(1)} all-reduce(f32[1024]{0:T(1024)S(1)} %dynamic-update-slice), channel_id=2, replica_groups=mesh['ep'=4,'tm'=32] {'tm'}, use_global_device_ids=true, to_apply=%add.1 | all-reduce | flops 1024 | bytes 8192
  91.3 1.3 while.52
  92.6 9.4 %fusion.43 = (f32[4,8,256,128]{3,1,2,0:T(8,128)S(1)}, f32[4,256,8,128]{3,2,1,0:T(8,128)}, f32[4,256,8,128]{3,2,1,0:T(8,128)}, f32[4,8,256,128]{3,1,2,0:T(8,128)}) fusion(f32[32]{0:T(128)S(1)} %get-tuple-element.296, f32[256,4,8,128]{3,2,1,0:T(8,128)} %copy-done.3, s32[32,32768]{1,0:T(8,128)} %param.14), kind=kLoop, calls=%fused_computation.98 | loop fusion | flops 5242880 | bytes 25165952
  102.8 1.1 bitcast_reduce_fusion
  105.6 4.4 reduce_window_min.10
  110.1 10.0 %fusion.20 = f32[256,4,8,128]{3,2,1,0:T(8,128)S(1)} fusion(f32[4,256,8,128]{3,2,1,0:T(8,128)} %get-tuple-element.384, s32[256,128]{1,0:T(8,128)S(1)} %copy.34, f32[32,256]{0,1:T(8,128)S(1)} %copy.50), kind=kOutput, calls=%fused_computation.47 | convolution fusion | flops 1615855616 | bytes 8552448 | tf_op jit(solution)/shard_map/ebj,bji->ebi/dot_general | solution.py:60
  120.4 1.8 copy-done.1
  122.4 1.4 copy-done.4
  124.6 1.1 bitcast_reduce_fusion.1
  126.7 10.2 %fusion.21 = f32[256,4,8,128]{3,2,1,0:T(8,128)S(1)} fusion(f32[4,256,8,128]{3,2,1,0:T(8,128)} %get-tuple-element.385, s32[256,128]{1,0:T(8,128)S(1)} %copy.34, f32[32,256]{0,1:T(8,128)S(1)} %copy.45), kind=kOutput, calls=%fused_computation.49 | convolution fusion | flops 1615855616 | bytes 8552448 | tf_op jit(solution)/shard_map/ebj,bji->ebi/dot_general | solution.py:60
  137.2 1.7 copy-done.2
  139.5 63.7 %all-reduce.4 = (f32[1024]{0:T(1024)S(1)}, f32[1024]{0:T(1024)S(1)}) all-reduce(f32[1024]{0:T(1024)S(1)} %dynamic-update-slice.1, f32[1024]{0:T(1024)S(1)} %dynamic-update-slice.2), channel_id=3, replica_groups=mesh['ep'=4,'tm'=32] {'tm'}, use_global_device_ids=true, to_apply=%add.2 | all-reduce | flops 2048 | bytes 16384
  203.4 10.7 %convert_bitcast_fusion = (bf16[1,32,32768]{2,1,0:T(8,128)(2,1)S(1)}, f32[32,32768]{1,0:T(8,128)}, bf16[1,32,32768]{2,1,0:T(8,128)(2,1)}, f32[32,32768]{1,0:T(8,128)}) fusion(f32[32]{0:T(128)S(1)} %get-tuple-element.298, f32[256,4,8,128]{3,2,1,0:T(8,128)} %copy-done.1, f32[32]{0:T(128)S(1)} %get-tuple-element.297, f32[256,4,8,128]{3,2,1,0:T(8,128)} %copy-done.2, ...), kind=kLoop, calls=%fused_computation.59 | loop fusion | flops 10485760 | bytes 29360384 | tf_op jit(solution)/shard_map/stack | solution.py:131
  214.1 3.1 fusion.30
  217.8 2.4 collective-permute-start.1
  220.7 117.9 %while.55 = (s32[]{:T(128)}, f32[32,2,64]{2,0,1:T(8,128)S(1)}, s32[32,32768]{1,0:T(8,128)}, f32[32,32768]{1,0:T(8,128)}, f32[32,32768]{1,0:T(8,128)}, /*index=5*/s32[]{:T(128)}, s32[]{:T(128)}, s32[]{:T(128)}, s32[]{:T(128)}) while((s32[]{:T(128)}, f32[32,2,64]{2,0,1:T(8,128)S(1)}, s32[32,32768]{1,0:T(8,128)}, ...), condition=%wide.region_18.19_spmd.clone, body=%wide.region_15.18_spmd.clone.sunk | while | flops 20979716 | bytes 2424989 | solution.py:89
  220.9 1.1 constant_dynamic-slice_fusion.8
  223.0 5.3 fusion.48
  228.3 1.1 constant_dynamic-slice_fusion.8
  230.3 5.3 fusion.48
  235.6 1.1 constant_dynamic-slice_fusion.8
  237.7 5.3 fusion.48
  243.0 1.1 constant_dynamic-slice_fusion.8
  245.0 5.3 fusion.48
  250.3 1.1 constant_dynamic-slice_fusion.8
  252.4 5.3 fusion.48
  259.8 5.3 fusion.48
  267.1 5.3 fusion.48
  274.5 5.3 fusion.48
  281.8 5.3 fusion.48
  289.2 5.3 fusion.48
  296.5 5.3 fusion.48
  303.9 5.3 fusion.48
  311.2 5.3 fusion.48
  318.6 5.3 fusion.48
  326.0 5.3 fusion.48
  333.3 5.3 fusion.48
  338.6 123.8 %psum.7 = f32[32,2,64]{2,0,1:T(8,128)S(1)} all-reduce(f32[32,2,64]{2,0,1:T(8,128)S(1)} %get-tuple-element.299), channel_id=1, replica_groups=mesh['ep'=4,'tm'=32] {'tm'}, use_global_device_ids=true, to_apply=%region_19.20 | all-reduce | flops 4096 | bytes 32768 | tf_op jit(solution)/shard_map/psum | solution.py:134
  462.4 2.3 broadcast_in_dim.128
  464.7 80.5 %while.54 = (s32[]{:T(128)}, f32[32,32768]{1,0:T(8,128)}, s32[32,32768]{1,0:T(8,128)}, f32[32,64]{1,0:T(8,128)S(1)}, s32[]{:T(128)}, /*index=5*/s32[]{:T(128)}, s32[]{:T(128)}, s32[]{:T(128)}) while((s32[]{:T(128)}, f32[32,32768]{1,0:T(8,128)}, s32[32,32768]{1,0:T(8,128)}, f32[32,64]{1,0:T(8,128)S(1)}, s32[]{:T(128)}, ...), condition=%wide.region_22.23_spmd.clone, body=%wide.region_20.22_spmd.clone.sunk | while | flops 12517382 | bytes 1581195 | solution.py:105
  465.6 3.3 select_reduce_fusion.2
  470.7 3.3 select_reduce_fusion.2
  475.7 3.3 select_reduce_fusion.2
  480.7 3.3 select_reduce_fusion.2
  485.8 3.3 select_reduce_fusion.2
  490.8 3.3 select_reduce_fusion.2
  495.8 3.3 select_reduce_fusion.2
  500.9 3.3 select_reduce_fusion.2
  505.9 3.3 select_reduce_fusion.2
  510.9 3.3 select_reduce_fusion.2
  515.9 3.3 select_reduce_fusion.2
  521.0 3.3 select_reduce_fusion.2
  526.0 3.3 select_reduce_fusion.2
  531.0 3.3 select_reduce_fusion.2
  536.1 3.3 select_reduce_fusion.2
  541.1 3.3 select_reduce_fusion.2
  545.1 2.5 broadcast_in_dim.135
  548.7 5.9 %add.189 = f32[32,32768]{1,0:T(8,128)} add(f32[32,32768]{1,0:T(8,128)} %param.12, f32[32,32768]{1,0:T(8,128)} %get-tuple-element.300) | non-fusion elementwise | flops 1048576 | bytes 12582912 | tf_op jit(solution)/shard_map/add | solution.py:136
  554.6 2.3 constant_dynamic-update-slice_fusion.3
  556.8 2.3 constant_dynamic-update-slice_fusion.1
  (182 shorter events, 67.8 us)
Async XLA Ops:
  6.1 2.5 copy-start.6
  19.0 2.0 copy-start.3
  19.0 2.1 copy-start.7
  120.1 2.1 copy-start.1
  120.1 3.7 copy-start.4
  136.9 2.0 copy-start.2
  217.2 337.3 %collective-permute-start = (bf16[2,32,1,8192]{3,1,2,0:T(8,128)(2,1)}, bf16[2,32,1,8192]{3,1,2,0:T(8,128)(2,1)}, u32[]{:S(2)}, u32[]{:S(2)}) collective-permute-start(bf16[2,32,1,8192]{3,1,2,0:T(8,128)(2,1)} %get-tuple-element.388), channel_id=1, source_target_pairs={{0,32},{32,0},{64,96},{96,64},{1,33},{33,1},{65,97},{97,65},{2,34}... | collective-permute-start | bytes 3145736 | tf_op jit(solution)/shard_map/ppermute | solution.py:21
  217.8 339.1 %collective-permute-start.1 = (bf16[2,32,1,8192]{3,1,2,0:T(8,128)(2,1)}, bf16[2,32,1,8192]{3,1,2,0:T(8,128)(2,1)}, u32[]{:S(2)}, u32[]{:S(2)}) collective-permute-start(bf16[2,32,1,8192]{3,1,2,0:T(8,128)(2,1)} %get-tuple-element.389), channel_id=1, source_target_pairs={{0,64},{32,96},{64,0},{96,32},{1,65},{33,97},{65,1},{97,33},{2,66}... | collective-permute-start | bytes 3145736 | tf_op jit(solution)/shard_map/ppermute | solution.py:21
  220.2 338.9 %collective-permute-start.2 = (bf16[2,32,1,8192]{3,1,2,0:T(8,128)(2,1)}, bf16[2,32,1,8192]{3,1,2,0:T(8,128)(2,1)S(1)}, u32[]{:S(2)}, u32[]{:S(2)}) collective-permute-start(bf16[2,32,1,8192]{3,1,2,0:T(8,128)(2,1)} %get-tuple-element.387), channel_id=1, source_target_pairs={{0,96},{32,64},{64,32},{96,0},{1,97},{33,65},{65,33},{97,1},{2,98}... | collective-permute-start | bytes 3145736 | tf_op jit(solution)/shard_map/ppermute | solution.py:21
  545.1 3.5 copy-start.5
  545.1 2.5 copy-start
